TPU v7x, 128 devices: a whole 4x4x4 slice. The times are simulated.
128 devices in a mesh: row: 8 (over y_lo, z), col: 16 (over x, y_hi, core).
Axes of the slice: x: 4, y: 4 (y_hi: 2, y_lo: 2; y = y_hi * 2 + y_lo), z: 4, core: 2. Of those that a mesh axis runs over, the one named last changes fastest.
Arguments:
- inverse: float32 [16384, 16384], P('row', 'col'), may hold values from -0.0625 to 0.0625
- pattern: int32 [128, 128], P('row', 'col'), may hold values 0 or 1
- factor_first: float32 [16384, 256], P('col'), may hold values from -1.5 to 1.5
- factor_second: float32 [16384, 256], P('col'), may hold values from -1.5 to 1.5
- rows_first: int32 [64], replicated, may hold values from 0 to 127, as said below
- rows_second: int32 [64], replicated, may hold values from 0 to 127, as said below
- coupling: float32 [256, 256], replicated, may hold values from -0.375 to 0.375
- diag_first: float32 [256, 256], replicated, may hold values from -6 to 6
- diag_second: float32 [256, 256], replicated, may hold values from -6 to 6
Outputs:
- panel_one: float32 [16384, 256], P(('row', 'col'))
- panel_two: float32 [16384, 256], P(('row', 'col'))
- block_one: float32 [256, 256], replicated
- block_cross: float32 [256, 256], replicated
- block_two: float32 [256, 256], replicated
Inputs may be any that keep to these rules, and one draw needn't show every extreme that they name: `rows_first`: 64 distinct block indices in increasing order; the first block, the block 64 and the last block are always among them. `rows_second`: 64 distinct block indices in increasing order; the first block, the block 64 and the last block are always among them.
All inputs are finite; a program needn't handle non-finite values. No bound on the sum of `pattern` on one device may be relied on, other than what follows from the above.
Results may differ from a plain program's by a relative error of at most 0.000071.
Values sent between devices are 32-bit elements; how exact they have to be, the bound alone decides.
A program may use at most 128 MiB of HBM per device.

v0:
```python
import jax
import jax.numpy as jnp
from jax import lax
from jax.sharding import PartitionSpec as P

BLK = 128


def member(block_ids, rows_list):
    hits = (block_ids[:, None] == rows_list[None, :]).astype(jnp.float32)
    return jnp.sum(hits, axis=1)


def per_device(
    inverse,
    pattern,
    factor_first,
    factor_second,
    rows_first,
    rows_second,
    coupling,
    diag_first,
    diag_second,
):
    high = lax.Precision.HIGHEST
    col_count = lax.axis_size("col")
    row_index = lax.axis_index("row")
    col_index = lax.axis_index("col")
    share_rows = factor_first.shape[0]
    local_rows, local_cols = inverse.shape
    quota_rows = local_rows // col_count
    masked = (
        inverse.reshape(local_rows // BLK, BLK, local_cols // BLK, BLK)
        * pattern.astype(jnp.float32)[:, None, :, None]
    ).reshape(local_rows, local_cols)
    share_ids = (col_index * share_rows + jnp.arange(share_rows, dtype=jnp.int32)) // BLK
    own_start = (row_index * col_count + col_index) * quota_rows
    own_ids = (own_start + jnp.arange(quota_rows, dtype=jnp.int32)) // BLK

    def fetch_rows(factor):
        gathered = lax.all_gather(factor, "col", axis=0, tiled=True)
        return lax.dynamic_slice_in_dim(gathered, own_start, quota_rows, 0)

    def panel_product(factor_kept):
        return lax.psum_scatter(
            jnp.dot(masked, factor_kept, precision=high), "col", scatter_dimension=0, tiled=True
        )

    x_one = factor_first * member(share_ids, rows_first)[:, None]
    x_two = factor_second * member(share_ids, rows_second)[:, None]
    panel_one = -panel_product(x_one)
    near_one = fetch_rows(factor_first)
    near_one = near_one * member(own_ids, rows_first)[:, None]
    first_total = lax.psum(jnp.dot(near_one.T, panel_one, precision=high), ("row", "col"))
    block_one = diag_first - first_total
    near_two = fetch_rows(factor_second)
    near_two = near_two * member(own_ids, rows_second)[:, None]
    panel_two = -(panel_product(x_two) + jnp.dot(panel_one, coupling, precision=high))
    cross_sum, quad_sum = lax.psum(
        (
            jnp.dot(panel_one.T, near_two, precision=high),
            jnp.dot(near_two.T, panel_two, precision=high),
        ),
        ("row", "col"),
    )
    block_cross = -(cross_sum + jnp.dot(block_one, coupling, precision=high))
    block_two = diag_second - quad_sum - jnp.dot(coupling.T, block_cross, precision=high)
    return (panel_one, panel_two, block_one, block_cross, block_two)


def solution(mesh):
    return jax.shard_map(
        per_device,
        mesh=mesh,
        in_specs=(
            P("row", "col"),
            P("row", "col"),
            P("col", None),
            P("col", None),
            P(),
            P(),
            P(),
            P(),
            P(),
        ),
        out_specs=(P(("row", "col"), None), P(("row", "col"), None), P(), P(), P()),
        check_vma=False,
    )
```

profile of v0, /device:TPU:1, one launch (start us, length us, event | category | flops | bytes accessed | tf_op | source)
XLA Modules:
  0.0 555.6 jit_solution(4285565588301605714)
XLA Ops:
  7.2 0.0 copy-start
  7.2 0.0 reduce-scatter.3.cloned.1.call-start
  7.2 0.7 convert_element_type.15
  7.9 0.1 copy.16
  8.0 1.0 convert_reduce_fusion
  9.0 0.6 mul.52
  9.6 0.0 copy-start.1
  9.6 3.8 copy-done.1
  13.4 0.1 copy-done.2
  13.5 10.3 %fusion.1 = f32[2048,256]{1,0:T(8,128)} fusion(f32[2048,1024]{1,0:T(8,128)S(1)} %copy-done.2, f32[256,8,8,128]{3,2,1,0:T(8,128)S(1)} %bitcast.19, f32[1024,256]{1,0:T(8,128)} %param.11, f32[1024]{0:T(1024)S(1)} %get-tuple-element.6), kind=kOutput, calls=%fused_computation.2 | convolution fusion | flops 6444810240 | bytes 19927040 | tf_op jit(solution)/shard_map/dot_general | solution.py:46
  23.8 0.0 reduce-scatter.3.cloned.1.call-update
  23.8 0.2 reduce-scatter.5.cloned.1.call-start
  24.0 0.0 copy-done.3
  24.0 0.0 copy-start.10
  24.0 0.0 copy-start.11
  24.1 0.0 copy-start.8
  24.1 12.9 %fusion = f32[2048,256]{1,0:T(8,128)} fusion(f32[2048,1024]{1,0:T(8,128)} %param.9, f32[256,8,8,128]{3,2,1,0:T(8,128)} %bitcast.20, f32[1024,256]{1,0:T(8,128)S(1)} %copy-done.3, f32[1024]{0:T(1024)S(1)} %get-tuple-element.5), kind=kOutput, calls=%fused_computation.1 | convolution fusion | flops 6444810240 | bytes 19927040 | tf_op jit(solution)/shard_map/dot_general | solution.py:46
  36.9 0.0 reduce-scatter.5.cloned.1.call-update
  37.0 0.0 all-gather.5.cloned.1.call-start
  37.0 0.7 all-gather.5.cloned.1.call-update
  37.7 0.0 all-gather.3.cloned.1.call-start
  37.8 0.5 all-gather.3.cloned.1.call-update
  38.3 0.0 all-reduce.3.cloned.1.call-start
  38.4 0.0 copy-done.10
  38.4 0.0 copy-done.11
  38.4 0.1 convert_reduce_fusion.2
  38.5 57.6 %reduce-scatter.3.cloned.1.call-done = f32[128,256]{1,0:T(8,128)} async-done(((f32[2048,256]{1,0:T(8,128)}), f32[128,256]{1,0:T(8,128)}) %reduce-scatter.3.cloned.1.call-update) | async-done | bytes 131088 | tf_op jit(solution)/shard_map/reduce_scatter | solution.py:45
  96.1 0.9 neg.9
  97.0 0.0 copy-start.4
  97.0 73.0 %reduce-scatter.5.cloned.1.call-done = f32[128,256]{1,0:T(8,128)} async-done(((f32[2048,256]{1,0:T(8,128)}), f32[128,256]{1,0:T(8,128)}) %reduce-scatter.5.cloned.1.call-update) | async-done | bytes 131088 | tf_op jit(solution)/shard_map/reduce_scatter | solution.py:45
  170.0 0.0 copy-done
  170.0 1.2 fusion.4
  171.2 0.0 copy-start.7
  171.2 112.4 %all-gather.5.cloned.1.call-done = f32[16384,256]{1,0:T(8,128)} async-done(((f32[1024,256]{1,0:T(8,128)}), f32[16384,256]{1,0:T(8,128)}) %all-gather.5.cloned.1.call-update) | async-done | bytes 16777232 | tf_op jit(solution)/shard_map/all_gather | solution.py:41
  283.5 2.1 fusion.13
  285.6 2.1 fusion.12
  287.7 105.6 %all-gather.3.cloned.1.call-done = f32[16384,256]{1,0:T(8,128)} async-done(((f32[1024,256]{1,0:T(8,128)}), f32[16384,256]{1,0:T(8,128)}) %all-gather.3.cloned.1.call-update) | async-done | bytes 16777232 | tf_op jit(solution)/shard_map/all_gather | solution.py:41
  393.3 2.1 fusion.9
  395.3 0.0 all-reduce.3.cloned.1.call-update
  395.4 148.9 %all-reduce.3.cloned.1.call-done = (f32[256,256]{1,0:T(8,128)}, f32[256,256]{1,0:T(8,128)}, f32[256,256]{1,0:T(8,128)}) async-done(((f32[256,256]{1,0:T(8,128)}, f32[256,256]{1,0:T(8,128)}, f32[256,256]{1,0:T(8,128)}), (f32[256,256]{1,0:T(8,128)}, f32[256,256]{1,0:T(8,128)}, f32[256,256]{1,0:T(8,128)})) %all-reduce.3.cloned.1.call-update) | async-done | bytes 786448 | tf_op jit(solution)/shard_map/psum | solution.py:54
  544.3 0.0 copy-done.8
  544.3 1.0 sub.23
  545.2 0.0 copy-start.5
  545.3 1.4 fusion.3
  546.7 0.0 copy-start.6
  546.7 0.0 copy-done.9
  546.7 2.3 fusion.2
  549.1 0.0 copy-done.6
  (8 shorter events, 0.0 us)
Async XLA Ops:
  7.2 162.8 %copy-start = (f32[256,256]{1,0:T(8,128)S(1)}, f32[256,256]{1,0:T(8,128)}, u32[]{:S(2)}) copy-start(f32[256,256]{1,0:T(8,128)} %param.15) | copy-start | bytes 786436
  7.2 88.9 %reduce-scatter.3.cloned.1.call-start = ((), (), s32[]{:S(2)}) async-start(), calls=%async_computation.2 | async-start | bytes 2228224 | tf_op jit(solution)/shard_map/reduce_scatter | solution.py:45
  8.0 5.5 copy-start.2
  9.6 3.8 copy-start.1
  13.5 10.5 %copy-start.3 = (f32[1024,256]{1,0:T(8,128)S(1)}, f32[1024,256]{1,0:T(8,128)}, u32[]{:S(2)}) copy-start(f32[1024,256]{1,0:T(8,128)} %param.12) | copy-start | bytes 3145732
  23.8 146.2 %reduce-scatter.5.cloned.1.call-start = ((), (), s32[]{:S(2)}) async-start(), calls=%async_computation.3 | async-start | bytes 2228224 | tf_op jit(solution)/shard_map/reduce_scatter | solution.py:45
  24.0 14.3 %copy-start.10 = (s32[64]{0:T(128)S(1)}, s32[64]{0:T(128)}, u32[]{:S(2)}) copy-start(s32[64]{0:T(128)} %param.14) | copy-start | bytes 772
  24.0 14.3 %copy-start.11 = (s32[64]{0:T(128)S(1)}, s32[64]{0:T(128)}, u32[]{:S(2)}) copy-start(s32[64]{0:T(128)} %param.13) | copy-start | bytes 772
  24.1 520.2 %copy-start.8 = (f32[256,256]{1,0:T(8,128)S(1)}, f32[256,256]{1,0:T(8,128)}, u32[]{:S(2)}) copy-start(f32[256,256]{1,0:T(8,128)} %param.16) | copy-start | bytes 786436
  36.9 509.8 %copy-start.9 = (f32[256,256]{1,0:T(8,128)S(1)}, f32[256,256]{1,0:T(8,128)}, u32[]{:S(2)}) copy-start(f32[256,256]{1,0:T(8,128)} %param.17) | copy-start | bytes 786436
  37.0 246.6 %all-gather.5.cloned.1.call-start = ((), (), s32[]{:S(2)}) async-start(), calls=%async_computation.5 | async-start | bytes 17825792 | tf_op jit(solution)/shard_map/all_gather | solution.py:41
  37.7 355.5 %all-gather.3.cloned.1.call-start = ((), (), s32[]{:S(2)}) async-start(), calls=%async_computation.4 | async-start | bytes 17825792 | tf_op jit(solution)/shard_map/all_gather | solution.py:41
  38.3 506.0 %all-reduce.3.cloned.1.call-start = ((), (), s32[]{:S(2)}) async-start(), calls=%async_computation.6 | async-start | bytes 1572864 | tf_op jit(solution)/shard_map/psum | solution.py:54
  97.0 452.1 %copy-start.4 = (f32[128,256]{1,0:T(8,128)}, f32[128,256]{1,0:T(8,128)S(1)}, u32[]{:S(2)}) copy-start(f32[128,256]{1,0:T(8,128)S(1)} %neg.9) | copy-start | bytes 393220
  171.2 377.9 %copy-start.7 = (f32[128,256]{1,0:T(8,128)}, f32[128,256]{1,0:T(8,128)S(1)}, u32[]{:S(2)}) copy-start(f32[128,256]{1,0:T(8,128)S(1)} %fusion.4) | copy-start | bytes 393220
  545.2 3.8 copy-start.5
  546.7 2.4 copy-start.6
Sparse Core Ops, SparseCore 0:
  23.9 72.0 reduce-scatter.2
  100.0 69.9 reduce-scatter.4
  172.4 111.1 all-gather.4
  285.8 107.4 all-gather.2
  398.7 145.5 all-reduce.2
where the time goes:
time: 556 us
  waiting for transfers between devices  499 us (90%)
  matrix products  34.3 us (6%)
  between operations  14 us (3%)
    all_gather x2, waiting for transfers between devices, fetch_rows(): gathered = lax.all_gather(factor, 'col', axis=0, tiled=True)  218 us
    psum x1, waiting for transfers between devices, per_device(): lax.psum(jnp.dot(near_one.T, panel_one, precision=high), ('row', 'col'))  149 us
    reduce_scatter x2, waiting for transfers between devices, panel_product(): lax.psum_scatter(jnp.dot(masked, factor_kept, precision=high), 'col', sca...  131 us
    dot_general x2, matrix products, panel_product(): jnp.dot(masked, factor_kept, precision=high)  23.1 us
  transfers between devices with their start and end apart: 5, of which 5 were waited for; matrix products, arithmetic and copies ran while one was open for 3% of the time, Pallas kernels for 0%

commit v1 on v0

--- a/solution.py
+++ b/solution.py
@@ -51,7 +51,7 @@
     panel_one = -panel_product(x_one)
     near_one = fetch_rows(factor_first)
     near_one = near_one * member(own_ids, rows_first)[:, None]
-    first_total = lax.psum(jnp.dot(near_one.T, panel_one, precision=high), ("row", "col"))
+    first_total = lax.psum(lax.psum(jnp.dot(near_one.T, panel_one, precision=high), "col"), "row")
     block_one = diag_first - first_total
     near_two = fetch_rows(factor_second)
     near_two = near_two * member(own_ids, rows_second)[:, None]

time: 556 us -> 773 us (1.39)
  waiting for transfers between devices: 499 us -> 715 us
    psum x1 -> x3, waiting for transfers between devices: 149 us -> 362 us  [the longest x1 156 us: per_device(): lax.psum((jnp.dot(panel_one.T, near_two, precision=high), jnp.dot(near_tw...]
    all_gather x2, waiting for transfers between devices: 218 us -> 226 us  [fetch_rows(): gathered = lax.all_gather(factor, 'col', axis=0, tiled=True)]
  transfers between devices with their start and end apart: 5 -> 7, of which waited for: 5 -> 7; matrix products, arithmetic and copies ran while one was open for 3% -> 3% of each run, Pallas kernels for 0% -> 0%
where the time goes in v1:
time: 773 us
  waiting for transfers between devices  715 us (92%)
  matrix products  34.1 us (4%)
  between operations  14.3 us (2%)
    all_gather x2, waiting for transfers between devices, fetch_rows(): gathered = lax.all_gather(factor, 'col', axis=0, tiled=True)  226 us
    psum x1, waiting for transfers between devices, per_device(): lax.psum((jnp.dot(panel_one.T, near_two, precision=high), jnp.dot(near_tw...  156 us
    psum x1, waiting for transfers between devices, per_device(): lax.psum(jnp.dot(near_one.T, panel_one, precision=high), 'col')  141 us
    reduce_scatter x2, waiting for transfers between devices, panel_product(): lax.psum_scatter(jnp.dot(masked, factor_kept, precision=high), 'col', sca...  126 us
    psum x1, waiting for transfers between devices, per_device(): lax.psum(lax.psum(jnp.dot(near_one.T, panel_one, precision=high), 'col'),...  65.2 us
    dot_general x2, matrix products, panel_product(): jnp.dot(masked, factor_kept, precision=high)  23.1 us
  transfers between devices with their start and end apart: 7, of which 7 were waited for; matrix products, arithmetic and copies ran while one was open for 3% of the time, Pallas kernels for 0%

profile of v1, /device:TPU:1, one launch (start us, length us, event | category | flops | bytes accessed | tf_op | source)
XLA Modules:
  0.0 772.6 jit_solution(5722496783620294308)
XLA Ops:
  7.2 0.0 copy-start
  7.2 0.0 reduce-scatter.3.cloned.1.call-start
  7.2 0.7 convert_element_type.15
  8.0 0.1 copy.16
  8.0 1.0 convert_reduce_fusion
  9.0 0.6 mul.52
  9.6 0.0 copy-start.1
  9.6 3.8 copy-done.1
  13.4 0.1 copy-done.2
  13.5 10.3 %fusion.1 = f32[2048,256]{1,0:T(8,128)} fusion(f32[2048,1024]{1,0:T(8,128)S(1)} %copy-done.2, f32[256,8,8,128]{3,2,1,0:T(8,128)S(1)} %bitcast.19, f32[1024,256]{1,0:T(8,128)} %param.11, f32[1024]{0:T(1024)S(1)} %get-tuple-element.6), kind=kOutput, calls=%fused_computation.2 | convolution fusion | flops 6444810240 | bytes 19927040 | tf_op jit(solution)/shard_map/dot_general | solution.py:46
  23.8 0.0 reduce-scatter.3.cloned.1.call-update
  23.8 0.0 all-gather.3.cloned.1.call-start
  23.8 0.7 all-gather.3.cloned.1.call-update
  24.5 0.2 reduce-scatter.5.cloned.1.call-start
  24.8 0.0 copy-start.10
  24.8 0.0 copy-start.11
  24.8 0.0 copy-start.8
  24.8 12.8 %fusion = f32[2048,256]{1,0:T(8,128)} fusion(f32[2048,1024]{1,0:T(8,128)} %param.9, f32[256,8,8,128]{3,2,1,0:T(8,128)} %bitcast.20, f32[1024,256]{1,0:T(8,128)S(1)} %copy-done.3, f32[1024]{0:T(1024)S(1)} %get-tuple-element.5), kind=kOutput, calls=%fused_computation.1 | convolution fusion | flops 6444810240 | bytes 19927040 | tf_op jit(solution)/shard_map/dot_general | solution.py:46
  37.6 0.0 reduce-scatter.5.cloned.1.call-update
  37.6 0.0 all-reduce.5.cloned.1.call-start
  37.7 0.1 convert_reduce_fusion.2
  37.8 58.2 %reduce-scatter.3.cloned.1.call-done = f32[128,256]{1,0:T(8,128)} async-done(((f32[2048,256]{1,0:T(8,128)}), f32[128,256]{1,0:T(8,128)}) %reduce-scatter.3.cloned.1.call-update) | async-done | bytes 131088 | tf_op jit(solution)/shard_map/reduce_scatter | solution.py:45
  96.0 0.9 neg.9
  96.9 0.0 copy-start.4
  96.9 112.6 %all-gather.3.cloned.1.call-done = f32[16384,256]{1,0:T(8,128)} async-done(((f32[1024,256]{1,0:T(8,128)}), f32[16384,256]{1,0:T(8,128)}) %all-gather.3.cloned.1.call-update) | async-done | bytes 16777232 | tf_op jit(solution)/shard_map/all_gather | solution.py:41
  209.6 2.1 fusion.9
  211.7 0.0 all-reduce.5.cloned.1.call-update
  211.7 0.0 all-gather.5.cloned.1.call-start
  211.7 0.5 all-gather.5.cloned.1.call-update
  212.3 0.0 all-reduce.7.cloned.1.call-start
  212.3 67.4 %reduce-scatter.5.cloned.1.call-done = f32[128,256]{1,0:T(8,128)} async-done(((f32[2048,256]{1,0:T(8,128)}), f32[128,256]{1,0:T(8,128)}) %reduce-scatter.5.cloned.1.call-update) | async-done | bytes 131088 | tf_op jit(solution)/shard_map/reduce_scatter | solution.py:45
  279.8 1.2 fusion.4
  281.0 0.0 copy-start.7
  281.0 141.4 %all-reduce.5.cloned.1.call-done = f32[256,256]{1,0:T(8,128)} async-done(((f32[256,256]{1,0:T(8,128)}), f32[256,256]{1,0:T(8,128)}) %all-reduce.5.cloned.1.call-update) | async-done | bytes 262160 | tf_op jit(solution)/shard_map/psum | solution.py:54
  422.4 0.0 all-reduce.7.cloned.1.call-update
  422.4 0.0 all-reduce.9.cloned.1.call-start
  422.5 113.5 %all-gather.5.cloned.1.call-done = f32[16384,256]{1,0:T(8,128)} async-done(((f32[1024,256]{1,0:T(8,128)}), f32[16384,256]{1,0:T(8,128)}) %all-gather.5.cloned.1.call-update) | async-done | bytes 16777232 | tf_op jit(solution)/shard_map/all_gather | solution.py:41
  536.0 2.1 fusion.13
  538.0 2.1 fusion.12
  540.1 0.0 all-reduce.9.cloned.1.call-update
  540.1 65.2 %all-reduce.7.cloned.1.call-done = f32[256,256]{1,0:T(8,128)} async-done(((f32[256,256]{1,0:T(8,128)}), f32[256,256]{1,0:T(8,128)}) %all-reduce.7.cloned.1.call-update) | async-done | bytes 262160 | tf_op jit(solution)/shard_map/psum | solution.py:54
  605.4 1.0 sub.23
  606.3 0.0 copy-start.5
  606.4 155.6 %all-reduce.9.cloned.1.call-done = (f32[256,256]{1,0:T(8,128)}, f32[256,256]{1,0:T(8,128)}) async-done(((f32[256,256]{1,0:T(8,128)}, f32[256,256]{1,0:T(8,128)}), (f32[256,256]{1,0:T(8,128)}, f32[256,256]{1,0:T(8,128)})) %all-reduce.9.cloned.1.call-update) | async-done | bytes 524304 | tf_op jit(solution)/shard_map/psum | solution.py:59
  762.0 1.3 fusion.3
  763.3 0.0 copy-start.6
  763.3 2.3 fusion.2
  765.7 0.0 copy-done.7
  (14 shorter events, 0.0 us)
Async XLA Ops:
  7.2 272.6 %copy-start = (f32[256,256]{1,0:T(8,128)S(1)}, f32[256,256]{1,0:T(8,128)}, u32[]{:S(2)}) copy-start(f32[256,256]{1,0:T(8,128)} %param.15) | copy-start | bytes 786436
  7.2 88.8 %reduce-scatter.3.cloned.1.call-start = ((), (), s32[]{:S(2)}) async-start(), calls=%async_computation.2 | async-start | bytes 2228224 | tf_op jit(solution)/shard_map/reduce_scatter | solution.py:45
  8.0 5.5 copy-start.2
  9.6 3.8 copy-start.1
  13.5 11.3 %copy-start.3 = (f32[1024,256]{1,0:T(8,128)S(1)}, f32[1024,256]{1,0:T(8,128)}, u32[]{:S(2)}) copy-start(f32[1024,256]{1,0:T(8,128)} %param.12) | copy-start | bytes 3145732
  23.8 185.8 %all-gather.3.cloned.1.call-start = ((), (), s32[]{:S(2)}) async-start(), calls=%async_computation.4 | async-start | bytes 17825792 | tf_op jit(solution)/shard_map/all_gather | solution.py:41
  24.5 255.2 %reduce-scatter.5.cloned.1.call-start = ((), (), s32[]{:S(2)}) async-start(), calls=%async_computation.3 | async-start | bytes 2228224 | tf_op jit(solution)/shard_map/reduce_scatter | solution.py:45
  24.8 12.9 %copy-start.10 = (s32[64]{0:T(128)S(1)}, s32[64]{0:T(128)}, u32[]{:S(2)}) copy-start(s32[64]{0:T(128)} %param.14) | copy-start | bytes 772
  24.8 12.9 %copy-start.11 = (s32[64]{0:T(128)S(1)}, s32[64]{0:T(128)}, u32[]{:S(2)}) copy-start(s32[64]{0:T(128)} %param.13) | copy-start | bytes 772
  24.8 580.6 %copy-start.8 = (f32[256,256]{1,0:T(8,128)S(1)}, f32[256,256]{1,0:T(8,128)}, u32[]{:S(2)}) copy-start(f32[256,256]{1,0:T(8,128)} %param.16) | copy-start | bytes 786436
  37.6 725.7 %copy-start.9 = (f32[256,256]{1,0:T(8,128)S(1)}, f32[256,256]{1,0:T(8,128)}, u32[]{:S(2)}) copy-start(f32[256,256]{1,0:T(8,128)} %param.17) | copy-start | bytes 786436
  37.6 384.8 %all-reduce.5.cloned.1.call-start = ((), (), s32[]{:S(2)}) async-start(), calls=%async_computation.5 | async-start | bytes 524288 | tf_op jit(solution)/shard_map/psum | solution.py:54
  96.9 668.8 %copy-start.4 = (f32[128,256]{1,0:T(8,128)}, f32[128,256]{1,0:T(8,128)S(1)}, u32[]{:S(2)}) copy-start(f32[128,256]{1,0:T(8,128)S(1)} %neg.9) | copy-start | bytes 393220
  211.7 324.3 %all-gather.5.cloned.1.call-start = ((), (), s32[]{:S(2)}) async-start(), calls=%async_computation.7 | async-start | bytes 17825792 | tf_op jit(solution)/shard_map/all_gather | solution.py:41
  212.3 393.1 %all-reduce.7.cloned.1.call-start = ((), (), s32[]{:S(2)}) async-start(), calls=%async_computation.6 | async-start | bytes 524288 | tf_op jit(solution)/shard_map/psum | solution.py:54
  281.0 484.7 %copy-start.7 = (f32[128,256]{1,0:T(8,128)}, f32[128,256]{1,0:T(8,128)S(1)}, u32[]{:S(2)}) copy-start(f32[128,256]{1,0:T(8,128)S(1)} %fusion.4) | copy-start | bytes 393220
  422.4 339.6 %all-reduce.9.cloned.1.call-start = ((), (), s32[]{:S(2)}) async-start(), calls=%async_computation.8 | async-start | bytes 1048576 | tf_op jit(solution)/shard_map/psum | solution.py:59
  606.3 159.3 %copy-start.5 = (f32[256,256]{1,0:T(8,128)}, f32[256,256]{1,0:T(8,128)S(1)}, u32[]{:S(2)}) copy-start(f32[256,256]{1,0:T(8,128)S(1)} %sub.23) | copy-start | bytes 786436
  763.3 2.4 copy-start.6
Sparse Core Ops, SparseCore 0:
  23.9 72.0 reduce-scatter.2
  98.4 111.1 all-gather.2
  213.5 66.1 reduce-scatter.4
  282.7 139.6 all-reduce.4
  424.6 111.2 all-gather.4
  538.3 67.0 all-reduce.6
  610.9 151.0 all-reduce.8
